TPU v7x, 32 devices: a whole 2x2x4 slice. The times are simulated.
32 devices in a mesh: dp: 8 (over y, x, core), code: 4 (over z).
Axes of the slice: x: 2, y: 2, z: 4, core: 2. Of those that a mesh axis runs over, the one named last changes fastest.
Arguments:
- temporal_out: bfloat16 [1024, 4096], P('dp'), may hold values from -6 to 6
- depth_in: bfloat16 [4, 4096, 1024], P('code', 'dp'), may hold values from -0.09375 to 0.09375
- embed: bfloat16 [4, 1024, 1024], P('code'), may hold values from -6 to 6
- depth_w1: bfloat16 [4, 1024, 2112], P('code', None, 'dp'), may hold values from -0.1875 to 0.1875
- depth_w2: bfloat16 [4, 1024, 2112], P('code', None, 'dp'), may hold values from -0.125 to 0.125
- audio_tokens: int32 [1024, 4], P(None, 'code'), may hold values from 0 to 1023
- barge_mask: int32 [1024], P('dp'), may hold values 0 or 1
- out_grad: bfloat16 [1024, 4, 1024], P('dp', 'code'), may hold values from -6 to 6
Outputs:
- temporal_grad: bfloat16 [1024, 4096], P('dp', 'code')
- depth_in_grad: bfloat16 [4, 4096, 1024], P('code', 'dp')
- embed_grad: bfloat16 [4, 1024, 1024], P('code', 'dp')
- w1_grad: bfloat16 [4, 1024, 2112], P('code', None, 'dp')
- w2_grad: bfloat16 [4, 1024, 2112], P('code', None, 'dp')
All inputs are finite; a program needn't handle non-finite values. No bound on the sum of `barge_mask` on one device may be relied on, other than what follows from the above.
Results may differ from a plain program's by a relative error of at most 0.02.
Values may be sent and summed in bfloat16 or wider, within the bound.
A program may use at most 128 MiB of HBM per device.

v0:
```python
import functools

import jax
import jax.numpy as jnp
from jax import lax
from jax.experimental import pallas as pl
from jax.experimental.pallas import tpu as pltpu
from jax.sharding import PartitionSpec as P

EPS = 1e-06
MESH = pl.DeviceIdType.MESH
CHUNKS = 2
TILE = 512


def dot_nt(left, right):
    return lax.dot_general(
        left, right, (((1,), (1,)), ((), ())), preferred_element_type=jnp.float32
    )


def dot_nn(left, right):
    return jnp.dot(left, right, preferred_element_type=jnp.float32)


def chain_kernel(
    n_dp,
    n_code,
    temporal,
    embedded,
    cot_ref,
    proj_own,
    w1_own,
    w2_own,
    temporal_grad,
    cols_all,
    normed_all,
    slope_all,
    carry_all,
    act_all,
    pre_all,
    proj,
    w1,
    w2,
    base,
    acc,
    incoming,
    returning,
    state,
    carry_out,
    deriv,
    act_t,
    pre_t,
    scale_ref,
    term,
    term_in,
    ring_send,
    ring_recv,
    pass_send,
    pass_recv,
    own_sem,
    chain_send,
    chain_recv,
    ag_send,
    ag_recv,
    swap_send,
    swap_recv,
    term_send,
    term_recv,
):
    dp = lax.axis_index("dp")
    code = lax.axis_index("code")
    rows, width = base.shape
    hidden = w1.shape[0]
    pad = hidden // n_dp
    depth = proj_own.shape[0]
    half = width // 2
    step_rows = rows // CHUNKS
    chips = n_dp // 2
    core = lax.rem(dp, 2)
    chip = dp // 2
    partner = chip * 2 + 1 - core

    def ring_place(c):
        return jnp.where(lax.rem(c, 2) == 0, c // 2, chips - 1 - c // 2)

    def ring_chip(p):
        p = lax.rem(p + 2 * chips, chips)
        return jnp.where(p < chips // 2, 2 * p, 2 * (chips - 1 - p) + 1)

    place = ring_place(chip)
    right = ring_chip(place + 1) * 2 + core
    left = ring_chip(place - 1) * 2 + core

    barrier = pltpu.get_barrier_semaphore()
    for other in range(1, n_dp):
        pl.semaphore_signal(
            barrier, inc=1, device_id=(lax.rem(dp + other, n_dp), code), device_id_type=MESH
        )
    for other in range(1, n_code):
        pl.semaphore_signal(
            barrier, inc=1, device_id=(dp, lax.rem(code + other, n_code)), device_id_type=MESH
        )
    pl.semaphore_wait(barrier, n_dp + n_code - 2)

    whole = (
        (proj_own, proj, depth),
        (w1_own, w1, pad),
        (w2_own, w2, pad),
    )

    def part(array, size, owner, way):
        start = pl.multiple_of(owner * size, 16)
        return array.at[pl.ds(start, size), pl.ds(way * half, half)]

    def ring_copy(i, way, step):
        own, full, size = whole[i]
        origin = ring_chip(place - step if way == 0 else place + step) * 2 + core
        dst = part(full, size, origin, way)
        src = own.at[:, pl.ds(way * half, half)] if step == 0 else dst
        return pltpu.make_async_remote_copy(
            src_ref=src,
            dst_ref=dst,
            send_sem=ring_send.at[i, way, step],
            recv_sem=ring_recv.at[i, way, step],
            device_id=(right if way == 0 else left, code),
            device_id_type=MESH,
        )

    def pass_copy(i, way, step):
        own, full, size = whole[i]
        origin = ring_chip(place - step if way == 0 else place + step) * 2 + core
        dst = part(full, size, origin, way)
        src = own.at[:, pl.ds(way * half, half)] if step == 0 else dst
        return pltpu.make_async_remote_copy(
            src_ref=src,
            dst_ref=dst,
            send_sem=pass_send.at[i, way, step],
            recv_sem=pass_recv.at[i, way, step],
            device_id=(partner, code),
            device_id_type=MESH,
        )

    def own_copy(i):
        own, full, size = whole[i]
        start = pl.multiple_of(dp * size, 16)
        return pltpu.make_async_copy(own, full.at[pl.ds(start, size), :], own_sem.at[i])

    def add_base(origin, way):
        lanes = pl.ds(way * half, half)
        base[:, lanes] += dot_nn(
            temporal[:, pl.ds(pl.multiple_of(origin * depth, 128), depth)],
            proj[pl.ds(pl.multiple_of(origin * depth, 16), depth), lanes],
        )

    for i in range(3):
        for way in range(2):
            ring_copy(i, way, 0).start()
    for i in range(3):
        for way in range(2):
            pass_copy(i, way, 0).start()
        own_copy(i).start()
    base[...] = embedded[...].astype(jnp.float32)
    own_copy(0).wait()
    for way in range(2):
        add_base(dp, way)
    for step in range(1, chips):
        for i in range(3):
            for way in range(2):
                ring_copy(i, way, step - 1).wait_recv()
                if step < chips - 1:
                    ring_copy(i, way, step).start()
                pass_copy(i, way, step).start()
            if i == 0:
                for way in range(2):
                    add_base(ring_chip(place - step if way == 0 else place + step) * 2 + core, way)
                for way in range(2):
                    pass_copy(0, way, step - 1).wait_recv()
                    add_base(
                        ring_chip(place - step + 1 if way == 0 else place + step - 1) * 2 + 1 - core,
                        way,
                    )
    for way in range(2):
        pass_copy(0, way, chips - 1).wait_recv()
        add_base(
            ring_chip(place - chips + 1 if way == 0 else place + chips - 1) * 2 + 1 - core, way
        )

    def swap_copy(i, other):
        target = lax.rem(dp + other, n_dp)
        if i == 0:
            src = temporal.at[:, pl.ds(pl.multiple_of(target * depth, 128), depth)]
            dst = cols_all.at[dp]
        else:
            table, full = ((act_t, act_all), (pre_t, pre_all))[i - 1]
            src = table.at[pl.ds(pl.multiple_of(target * pad, 16), pad), :]
            dst = full.at[dp]
        return pltpu.make_async_remote_copy(
            src_ref=src,
            dst_ref=dst,
            send_sem=swap_send.at[i, other],
            recv_sem=swap_recv.at[i, other],
            device_id=(target, code),
            device_id_type=MESH,
        )

    gathered = (normed_all, slope_all, carry_all)

    def peer_copy(i, other):
        block = gathered[i].at[dp]
        target = lax.rem(dp + 2 * other, n_dp)
        return pltpu.make_async_remote_copy(
            src_ref=block,
            dst_ref=block,
            send_sem=ag_send.at[i, 0, other],
            recv_sem=ag_recv.at[i, 0, other],
            device_id=(target, code),
            device_id_type=MESH,
        )

    def hand_copy(i, other):
        block = gathered[i].at[lax.rem(dp - 2 * other + n_dp, n_dp)]
        return pltpu.make_async_remote_copy(
            src_ref=block,
            dst_ref=block,
            send_sem=ag_send.at[i, 1, other],
            recv_sem=ag_recv.at[i, 1, other],
            device_id=(partner, code),
            device_id_type=MESH,
        )

    def gather_start(i):
        for other in range(1, chips):
            peer_copy(i, other).start()
        hand_copy(i, 0).start()

    def gather_forward(i):
        for other in range(1, chips):
            peer_copy(i, other).wait_recv()
            hand_copy(i, other).start()

    def gather_finish(i):
        for other in range(1, chips):
            peer_copy(i, other).wait_send()
        for other in range(chips):
            hand_copy(i, other).wait()

    def chain_copy(way, c):
        chunk = pl.ds(c * step_rows, step_rows)
        src, dst = ((state, incoming), (carry_out, returning))[way]
        target = lax.rem(code + (1 if way == 0 else n_code - 1), n_code)
        return pltpu.make_async_remote_copy(
            src_ref=src.at[chunk, :],
            dst_ref=dst.at[chunk, :],
            send_sem=chain_send.at[way, c],
            recv_sem=chain_recv.at[way, c],
            device_id=(dp, target),
            device_id_type=MESH,
        )

    first = code == 0
    last = code == n_code - 1

    @pl.when(first)
    def _():
        incoming[...] = jnp.zeros_like(incoming)

    @pl.when(last)
    def _():
        returning[...] = jnp.zeros_like(returning)

    for i in range(1, 3):
        own_copy(i).wait()
        for way in range(2):
            for step in range(chips):
                pass_copy(i, way, step).wait_recv()
    for other in range(1, n_dp):
        swap_copy(0, other).start()
    cols_all[dp] = temporal[:, pl.ds(pl.multiple_of(dp * depth, 128), depth)]

    tiles = hidden // TILE
    rest = hidden - tiles * TILE

    def over_tiles(body):
        def turn(t, carry):
            body(pl.multiple_of(t * TILE, TILE), TILE)
            return carry

        lax.fori_loop(0, tiles, turn, 0)
        if rest:
            body(tiles * TILE, rest)

    for c in range(CHUNKS):
        chunk = pl.ds(c * step_rows, step_rows)

        @pl.when(jnp.logical_not(first))
        def _():
            chain_copy(0, c).wait_recv()

        resid = base[chunk, :] + incoming[chunk, :].astype(jnp.float32)
        base[chunk, :] = resid
        scale = lax.rsqrt(jnp.mean(resid * resid, axis=-1, keepdims=True) + EPS)
        scale_ref[chunk, :] = jnp.broadcast_to(scale, (step_rows, 128))
        normed_all[dp, chunk, :] = (resid * scale).astype(jnp.bfloat16)
        acc[chunk, :] = resid

        def forward(start, size):
            lanes = pl.ds(start, size)
            pre = dot_nt(normed_all[dp, chunk, :], w1[lanes, :])
            deriv[chunk, lanes] = pre
            active = (pre * jax.nn.sigmoid(pre)).astype(jnp.bfloat16)
            acc[chunk, :] += dot_nn(active, w2[lanes, :])

        over_tiles(forward)
        state[chunk, :] = acc[chunk, :].astype(jnp.bfloat16)

        @pl.when(jnp.logical_not(last))
        def _():
            chain_copy(0, c).start()

    gather_start(0)

    def slopes(start, size):
        lanes = pl.ds(start, size)
        pre = deriv[:, lanes]
        sigma = jax.nn.sigmoid(pre)
        active = pre * sigma
        deriv[:, lanes] = sigma * (1.0 + pre * (1.0 - sigma))
        act_t[lanes, :] = active.T.astype(jnp.bfloat16)

    over_tiles(slopes)
    for other in range(1, n_dp):
        swap_copy(1, other).start()
    act_all[dp] = act_t[pl.ds(pl.multiple_of(dp * pad, 16), pad), :]

    @pl.when(first)
    def _():
        gather_forward(0)


    for c in range(CHUNKS):
        chunk = pl.ds(c * step_rows, step_rows)

        @pl.when(jnp.logical_not(last))
        def _():
            chain_copy(1, c).wait_recv()

        slope = cot_ref[chunk, :].astype(jnp.float32) + returning[chunk, :].astype(jnp.float32)
        slope_all[dp, chunk, :] = slope.astype(jnp.bfloat16)
        if c == CHUNKS - 1:
            gather_start(1)
        acc[chunk, :] = jnp.zeros((step_rows, width), jnp.float32)

        def backward(start, size):
            lanes = pl.ds(start, size)
            back = dot_nt(slope_all[dp, chunk, :], w2[lanes, :])
            pre_slope = back * deriv[chunk, lanes]
            deriv[chunk, lanes] = pre_slope
            acc[chunk, :] += dot_nn(pre_slope.astype(jnp.bfloat16), w1[lanes, :])

        over_tiles(backward)
        norm_slope = acc[chunk, :]
        scale = scale_ref[chunk, 0:1]
        unit = base[chunk, :] * scale
        slope = cot_ref[chunk, :].astype(jnp.float32) + returning[chunk, :].astype(jnp.float32)
        carried = (
            slope
            + scale * (norm_slope - unit * jnp.mean(norm_slope * unit, axis=-1, keepdims=True))
        ).astype(jnp.bfloat16)
        carry_out[chunk, :] = carried
        carry_all[dp, chunk, :] = carried

        @pl.when(jnp.logical_not(first))
        def _():
            chain_copy(1, c).start()

    gather_start(2)

    @pl.when(jnp.logical_not(first))
    def _():
        gather_forward(0)

    quarter = term.shape[2]
    per = quarter // depth
    early = code * 2 < n_code

    def term_copy(other):
        target = lax.rem(code + other, n_code)
        return pltpu.make_async_remote_copy(
            src_ref=term.at[target],
            dst_ref=term_in.at[other],
            send_sem=term_send.at[other],
            recv_sem=term_recv.at[other],
            device_id=(dp, target),
            device_id_type=MESH,
        )

    for other in reversed(range(n_code)):
        target = lax.rem(code + other, n_code)
        for piece in range(per):
            start = pl.multiple_of(target * quarter + piece * depth, 16)
            term[target, :, piece * depth : (piece + 1) * depth] = dot_nt(
                carry_all[dp], proj[pl.ds(start, depth), :]
            ).astype(jnp.bfloat16)
        if other:

            @pl.when(early)
            def _():
                term_copy(other).start()

    def turn_over(start, size):
        lanes = pl.ds(start, size)
        pre_t[lanes, :] = deriv[:, lanes].T.astype(jnp.bfloat16)

    over_tiles(turn_over)
    for other in range(1, n_dp):
        swap_copy(2, other).start()
    pre_all[dp] = pre_t[pl.ds(pl.multiple_of(dp * pad, 16), pad), :]

    gather_forward(1)
    gather_forward(2)

    @pl.when(jnp.logical_not(early))
    def _():
        for other in range(1, n_code):
            term_copy(other).start()

    total = term[code].astype(jnp.float32)
    for other in range(1, n_code):
        term_copy(other).wait_recv()
        total += term_in[other].astype(jnp.float32)
    temporal_grad[...] = total.astype(jnp.bfloat16)

    for i in range(3):
        for way in range(2):
            for step in range(chips - 1):
                ring_copy(i, way, step).wait_send()
            for step in range(chips):
                pass_copy(i, way, step).wait_send()
    for c in range(CHUNKS):

        @pl.when(jnp.logical_not(last))
        def _():
            chain_copy(0, c).wait_send()

        @pl.when(jnp.logical_not(first))
        def _():
            chain_copy(1, c).wait_send()

    for i in range(3):
        gather_finish(i)
        for other in range(1, n_dp):
            swap_copy(i, other).wait()
    for other in range(1, n_code):
        term_copy(other).wait_send()


def per_device(
    temporal_out, depth_in, embed, depth_w1, depth_w2, audio_tokens, barge_mask, out_grad
):
    dp_index = lax.axis_index("dp")
    n_code = lax.axis_size("code")
    n_dp = lax.axis_size("dp")
    rows, wide = temporal_out.shape
    depth, width = depth_in.shape[1:]
    share = depth_w1.shape[2]
    pad = -(-share // 16) * 16
    hidden = pad * n_dp
    quarter = wide // n_code
    chips = n_dp // 2
    table = embed[0]
    token_all = audio_tokens[:, 0]
    token_own = lax.dynamic_slice_in_dim(token_all, dp_index * rows, rows, 0)
    embedded = jnp.take(table, token_own, axis=0)
    cotangent = out_grad[:, 0, :] * barge_mask.astype(jnp.bfloat16)[:, None]
    w1_own = jnp.pad(depth_w1[0].T, ((0, pad - share), (0, 0)))
    w2_own = jnp.pad(depth_w2[0].T, ((0, pad - share), (0, 0)))

    bf16, f32 = jnp.bfloat16, jnp.float32
    vmem = pl.BlockSpec(memory_space=pltpu.VMEM)
    hbm = pl.BlockSpec(memory_space=pl.ANY)
    dma = pltpu.SemaphoreType.DMA
    out_shape = (
        jax.ShapeDtypeStruct((rows, quarter), bf16),
        jax.ShapeDtypeStruct((n_dp, rows, depth), bf16),
        jax.ShapeDtypeStruct((n_dp, rows, width), bf16),
        jax.ShapeDtypeStruct((n_dp, rows, width), bf16),
        jax.ShapeDtypeStruct((n_dp, rows, width), bf16),
        jax.ShapeDtypeStruct((n_dp, pad, rows), bf16),
        jax.ShapeDtypeStruct((n_dp, pad, rows), bf16),
    )
    temporal_grad, cols_all, normed_all, slope_all, carry_all, act_all, pre_all = pl.pallas_call(
        functools.partial(chain_kernel, n_dp, n_code),
        out_shape=out_shape,
        in_specs=[vmem, vmem, vmem, hbm, hbm, hbm],
        out_specs=(vmem,) * 7,
        scratch_shapes=[
            pltpu.VMEM((wide, width), bf16),
            pltpu.VMEM((hidden, width), bf16),
            pltpu.VMEM((hidden, width), bf16),
            pltpu.VMEM((rows, width), f32),
            pltpu.VMEM((rows, width), f32),
            pltpu.VMEM((rows, width), bf16),
            pltpu.VMEM((rows, width), bf16),
            pltpu.VMEM((rows, width), bf16),
            pltpu.VMEM((rows, width), bf16),
            pltpu.VMEM((rows, hidden), f32),
            pltpu.VMEM((hidden, rows), bf16),
            pltpu.VMEM((hidden, rows), bf16),
            pltpu.VMEM((rows, 128), f32),
            pltpu.VMEM((n_code, rows, quarter), bf16),
            pltpu.VMEM((n_code, rows, quarter), bf16),
            dma((3, 2, chips)),
            dma((3, 2, chips)),
            dma((3, 2, chips)),
            dma((3, 2, chips)),
            dma((3,)),
            dma((2, CHUNKS)),
            dma((2, CHUNKS)),
            dma((3, 2, chips)),
            dma((3, 2, chips)),
            dma((3, n_dp)),
            dma((3, n_dp)),
            dma((n_code,)),
            dma((n_code,)),
        ],
        compiler_params=pltpu.CompilerParams(
            collective_id=0, has_side_effects=True, vmem_limit_bytes=60 * 1024 * 1024
        ),
        name="depth_chain",
    )(temporal_out, embedded, cotangent, depth_in[0], w1_own, w2_own)

    def over_rows(left, right):
        return lax.dot_general(
            left, right, (((0,), (0,)), ((), ())), preferred_element_type=jnp.float32
        )

    frames = n_dp * rows
    normed = normed_all.reshape(frames, width)
    slope = slope_all.reshape(frames, width)
    carry = carry_all.reshape(frames, width)
    columns = cols_all.reshape(frames, depth)
    pre_rows = pre_all[:, :share, :].transpose(0, 2, 1).reshape(frames, share)
    act_rows = act_all[:, :share, :].transpose(0, 2, 1).reshape(frames, share)
    first_grad = over_rows(normed, pre_rows).astype(bf16)
    second_grad = over_rows(slope, act_rows).astype(bf16)
    proj_grad = over_rows(columns, carry).astype(bf16)
    vocab_local = table.shape[0] // n_dp
    vocab_ids = lax.broadcasted_iota(jnp.int32, (1, vocab_local), 1) + dp_index * vocab_local
    onehot = (token_all[:, None] == vocab_ids).astype(bf16)
    table_grad = over_rows(onehot, carry).astype(bf16)
    return (
        temporal_grad,
        proj_grad[None],
        table_grad[None],
        first_grad[None],
        second_grad[None],
    )


def solution(mesh):
    in_specs = (
        P("dp", None),
        P("code", "dp", None),
        P("code", None, None),
        P("code", None, "dp"),
        P("code", None, "dp"),
        P(None, "code"),
        P("dp"),
        P("dp", "code", None),
    )
    out_specs = (
        P("dp", "code"),
        P("code", "dp", None),
        P("code", "dp", None),
        P("code", None, "dp"),
        P("code", None, "dp"),
    )
    return jax.shard_map(
        per_device, mesh=mesh, in_specs=in_specs, out_specs=out_specs, check_vma=False
    )
```

profile of v0, /device:TPU:0, one launch (start us, length us, event | category | flops | bytes accessed | tf_op | source)
XLA Modules:
  0.0 190.9 jit_solution(5976119653033050206)
XLA Ops:
  0.6 0.0 copy-start
  0.6 0.0 copy-start.3
  0.7 1.6 copy-done
  2.2 0.7 convert_element_type.19
  2.9 0.7 and_bitcast_fusion
  3.6 0.0 copy-start.4
  3.6 0.9 gather_fusion
  4.4 1.8 bitcast_multiply_fusion
  6.3 0.0 copy-done.3
  6.3 0.8 pad.7.w1_own
  7.1 0.0 copy-done.4
  7.1 0.9 pad.8.w2_own
  8.0 0.0 copy-start.6
  8.0 172.0 %depth_chain.1 = (bf16[128,1024]{1,0:T(8,128)(2,1)}, bf16[8,128,512]{2,1,0:T(8,128)(2,1)}, bf16[8,128,1024]{2,1,0:T(8,128)(2,1)}, bf16[8,128,1024]{2,1,0:T(8,128...) custom-call(bf16[128,4096]{1,0:T(8,128)(2,1)} %temporal.1, ...), custom_call_target="tpu_custom_call" | custom-call | tf_op jit(solution)/shard_map/depth_chain/pallas_call | solution.py:492
  180.0 0.0 copy-start.8
  180.0 0.0 copy-done.6
  180.0 3.1 %fusion.5 = bf16[1,128,1024]{2,1,0:T(8,128)(2,1)} fusion(bf16[1024,1024]{1,0:T(8,128)(2,1)} %bitcast.51, s32[128]{0:T(128)S(1)} %iota_add_fusion, s32[1024]{0:T(1024)S(1)} %bitcast.55), kind=kOutput, calls=%fused_computation.10 | convolution fusion | flops 268697600 | bytes 2363904 | tf_op jit(solution)/shard_map/dot_general | solution.py:534
  183.1 0.0 copy-done.8
  183.1 0.0 copy-start.7
  183.1 0.0 copy-start.9
  183.1 2.7 %fusion.4 = bf16[1,1024,264]{1,2,0:T(8,128)(2,1)} fusion(bf16[8,128,1024]{2,1,0:T(8,128)(2,1)S(1)} %copy-done.8, bf16[8,272,128]{2,1,0:T(8,128)(2,1)} %get-tuple-element.16), kind=kOutput, calls=%fused_computation.8 | convolution fusion | flops 553918464 | bytes 3178496 | tf_op jit(solution)/shard_map/dot_general | solution.py:534
  185.8 0.0 copy-done.7
  185.8 0.0 copy-done.9
  185.9 0.0 copy-start.1
  185.9 0.0 copy-start.2
  185.9 1.5 fusion.3
  187.4 0.0 copy-done.1
  187.4 0.5 copy-done.2
  187.9 0.0 copy-start.5
  187.9 2.2 %fusion = bf16[1,512,1024]{2,1,0:T(8,128)(2,1)} fusion(bf16[8,128,512]{2,1,0:T(8,128)(2,1)S(1)} %copy-done.2, bf16[8,128,1024]{2,1,0:T(8,128)(2,1)S(1)} %copy-done.1), kind=kOutput, calls=%fused_computation.4 | convolution fusion | flops 1074266112 | bytes 4194304 | tf_op jit(solution)/shard_map/dot_general | solution.py:534
  190.1 0.0 copy-done.5
  190.2 0.7 copy.16
  (2 shorter events, 0.0 us)
Async XLA Ops:
  0.6 1.6 copy-start
  0.6 5.6 %copy-start.3 = (bf16[1,1024,264]{1,2,0:T(8,128)(2,1)S(1)}, bf16[1,1024,264]{1,2,0:T(8,128)(2,1)}, u32[]{:S(2)}) copy-start(bf16[1,1024,264]{1,2,0:T(8,128)(2,1)} %param.11) | copy-start | bytes 1622020
  3.6 3.6 %copy-start.4 = (bf16[1,1024,264]{1,2,0:T(8,128)(2,1)S(1)}, bf16[1,1024,264]{1,2,0:T(8,128)(2,1)}, u32[]{:S(2)}) copy-start(bf16[1,1024,264]{1,2,0:T(8,128)(2,1)} %param.12) | copy-start | bytes 1622020
  8.0 172.0 %copy-start.6 = (s32[1024,1]{0,1:T(1,128)S(1)}, s32[1024,1]{0,1:T(1,128)}, u32[]{:S(2)}) copy-start(s32[1024,1]{0,1:T(1,128)} %param.13) | copy-start | bytes 12292
  180.0 3.1 %copy-start.8 = (bf16[8,128,1024]{2,1,0:T(8,128)(2,1)S(1)}, bf16[8,128,1024]{2,1,0:T(8,128)(2,1)}, u32[]{:S(2)}) copy-start(bf16[8,128,1024]{2,1,0:T(8,128)(2,1)} %get-tuple-element.15) | copy-start | bytes 6291460
  183.1 2.7 %copy-start.7 = (bf16[8,128,1024]{2,1,0:T(8,128)(2,1)S(1)}, bf16[8,128,1024]{2,1,0:T(8,128)(2,1)}, u32[]{:S(2)}) copy-start(bf16[8,128,1024]{2,1,0:T(8,128)(2,1)} %get-tuple-element.17) | copy-start | bytes 6291460
  183.1 2.7 %copy-start.9 = (bf16[8,272,128]{2,1,0:T(8,128)(2,1)S(1)}, bf16[8,272,128]{2,1,0:T(8,128)(2,1)}, u32[]{:S(2)}) copy-start(bf16[8,272,128]{2,1,0:T(8,128)(2,1)} %get-tuple-element.18) | copy-start | bytes 1671172
  185.9 1.6 copy-start.1
  185.9 2.1 %copy-start.2 = (bf16[8,128,512]{2,1,0:T(8,128)(2,1)S(1)}, bf16[8,128,512]{2,1,0:T(8,128)(2,1)}, u32[]{:S(2)}) copy-start(bf16[8,128,512]{2,1,0:T(8,128)(2,1)} %get-tuple-element.13) | copy-start | bytes 3145732
  187.9 2.2 %copy-start.5 = (bf16[128,1024]{1,0:T(8,128)(2,1)S(1)}, bf16[128,1024]{1,0:T(8,128)(2,1)}, u32[]{:S(2)}) copy-start(bf16[128,1024]{1,0:T(8,128)(2,1)} %get-tuple-element.28) | copy-start | bytes 786436
where the time goes:
time: 192 us; the launch traced here: 191 us
  Pallas kernels  172 us (90%)
  matrix products  9.63 us (5%)
  local copies, waits for them, and re-layouts  5.36 us (3%)
  other arithmetic  3.16 us (2%)
    pallas_call x1, Pallas kernels, per_device(): pl.pallas_call(functools.partial(chain_kernel, n_dp, n_code), out_shape=o...  172 us
    dot_general x4, matrix products, over_rows(): lax.dot_general(left, right, (((0,), (0,)), ((), ())), preferred_element_...  9.63 us

commit v1 on v0

v1 whole, which is shorter than its diff:
```python
import functools

import jax
import jax.numpy as jnp
from jax import lax
from jax.experimental import pallas as pl
from jax.experimental.pallas import tpu as pltpu
from jax.sharding import PartitionSpec as P

EPS = 1e-06
MESH = pl.DeviceIdType.MESH
CHUNKS = 4
BF16, F32 = jnp.bfloat16, jnp.float32


def dot_nn(left, right):
    return jnp.dot(left, right, preferred_element_type=F32)


def dot_tn(left, right):
    return lax.dot_general(left, right, (((0,), (0,)), ((), ())), preferred_element_type=F32)


def chain_kernel(
    n_dp,
    n_code,
    temporal_hbm,
    cot_hbm,
    table_hbm,
    token_hbm,
    mask_hbm,
    proj_own,
    w1_own,
    w2_own,
    temporal_grad,
    proj_grad,
    table_grad,
    w1_grad,
    w2_grad,
    temporal,
    cot_ref,
    token,
    mask,
    proj,
    w1,
    w2,
    proj_t,
    w1_t,
    w2_t,
    base,
    incoming,
    returning,
    state,
    pre_ref,
    act,
    slope_h,
    act_t,
    pre_t,
    scale_ref,
    term,
    term_in,
    cols_all,
    normed_all,
    slope_all,
    carry_all,
    act_all,
    pre_all,
    load_sem,
    ring_send,
    ring_recv,
    pass_send,
    pass_recv,
    own_sem,
    chain_send,
    chain_recv,
    ag_send,
    ag_recv,
    swap_send,
    swap_recv,
    term_send,
    term_recv,
):
    dp = lax.axis_index("dp")
    code = lax.axis_index("code")
    rows, width = base.shape
    hidden = w1.shape[0]
    pad = hidden // n_dp
    share = w1_grad.shape[0]
    used = w1_own.shape[0]
    depth = proj_own.shape[0]
    half = width // 2
    step_rows = rows // CHUNKS
    chips = n_dp // 2
    core = lax.rem(dp, 2)
    chip = dp // 2
    partner = chip * 2 + 1 - core
    first = code == 0
    last = code == n_code - 1

    def ring_place(c):
        return jnp.where(lax.rem(c, 2) == 0, c // 2, chips - 1 - c // 2)

    def ring_chip(p):
        p = lax.rem(p + 2 * chips, chips)
        return jnp.where(p < chips // 2, 2 * p, 2 * (chips - 1 - p) + 1)

    place = ring_place(chip)
    right = ring_chip(place + 1) * 2 + core
    left = ring_chip(place - 1) * 2 + core

    loads = [
        pltpu.make_async_copy(src, dst, load_sem.at[i])
        for i, (src, dst) in enumerate(
            (
                (temporal_hbm, temporal),
                (cot_hbm, cot_ref),
                (table_hbm, w2_t.at[pl.ds(0, table_hbm.shape[0]), pl.ds(0, width)]),
                (token_hbm, token),
                (mask_hbm, mask),
            )
        )
    ]

    barrier = pltpu.get_barrier_semaphore()
    for other in range(1, n_dp):
        pl.semaphore_signal(
            barrier, inc=1, device_id=(lax.rem(dp + other, n_dp), code), device_id_type=MESH
        )
    for other in range(1, n_code):
        pl.semaphore_signal(
            barrier, inc=1, device_id=(dp, lax.rem(code + other, n_code)), device_id_type=MESH
        )
    for load in loads:
        load.start()
    if pad > used:
        for owner in range(n_dp):
            fill = jnp.zeros((pad - used, width), BF16)
            w1[owner * pad + used : (owner + 1) * pad, :] = fill
            w2[owner * pad + used : (owner + 1) * pad, :] = fill
    pl.semaphore_wait(barrier, n_dp + n_code - 2)

    whole = (
        (proj_own, proj, depth, depth),
        (w1_own, w1, pad, used),
        (w2_own, w2, pad, used),
    )

    def part(i, owner, way):
        _, full, size, filled = whole[i]
        start = pl.multiple_of(owner * size, 16)
        return full.at[pl.ds(start, filled), pl.ds(way * half, half)]

    def origin_of(way, step):
        return ring_chip(place - step if way == 0 else place + step) * 2 + core

    def ring_copy(i, way, step):
        dst = part(i, origin_of(way, step), way)
        src = whole[i][0].at[:, pl.ds(way * half, half)] if step == 0 else dst
        return pltpu.make_async_remote_copy(
            src_ref=src,
            dst_ref=dst,
            send_sem=ring_send.at[i, way, step],
            recv_sem=ring_recv.at[i, way, step],
            device_id=(right if way == 0 else left, code),
            device_id_type=MESH,
        )

    def pass_copy(i, way, step):
        dst = part(i, origin_of(way, step), way)
        src = whole[i][0].at[:, pl.ds(way * half, half)] if step == 0 else dst
        return pltpu.make_async_remote_copy(
            src_ref=src,
            dst_ref=dst,
            send_sem=pass_send.at[i, way, step],
            recv_sem=pass_recv.at[i, way, step],
            device_id=(partner, code),
            device_id_type=MESH,
        )

    def own_copy(i):
        own, full, size, filled = whole[i]
        start = pl.multiple_of(dp * size, 16)
        return pltpu.make_async_copy(own, full.at[pl.ds(start, filled), :], own_sem.at[i])

    def add_base(origin, way):
        lanes = pl.ds(way * half, half)
        spot = pl.ds(pl.multiple_of(origin * depth, 128), depth)
        block = proj[pl.ds(pl.multiple_of(origin * depth, 16), depth), lanes]
        base[:, lanes] += dot_nn(temporal[:, spot], block)
        proj_t[lanes, spot] = block.T

    def flip(source, target):
        def turn(t, carry):
            spot = pl.ds(pl.multiple_of(t * 128, 128), 128)
            target[:, spot] = source[spot, :].T
            return carry

        lax.fori_loop(0, hidden // 128, turn, 0)
        rest = hidden % 128
        if rest:
            target[:, hidden - rest :] = source[hidden - rest :, :].T

    def swap_copy(i, other):
        target = lax.rem(dp + other, n_dp)
        spot = pl.ds(pl.multiple_of(dp * rows, 128), rows)
        if i == 0:
            src = temporal.at[:, pl.ds(pl.multiple_of(target * depth, 128), depth)]
            dst = cols_all.at[dp]
        else:
            source, full = ((act_t, act_all), (pre_t, pre_all))[i - 1]
            src = source.at[pl.ds(pl.multiple_of(target * pad, 16), pad), :]
            dst = full.at[:, spot]
        return pltpu.make_async_remote_copy(
            src_ref=src,
            dst_ref=dst,
            send_sem=swap_send.at[i, other],
            recv_sem=swap_recv.at[i, other],
            device_id=(target, code),
            device_id_type=MESH,
        )

    gathered = (normed_all, slope_all, carry_all)

    def peer_copy(i, other):
        block = gathered[i].at[dp]
        target = lax.rem(dp + 2 * other, n_dp)
        return pltpu.make_async_remote_copy(
            src_ref=block,
            dst_ref=block,
            send_sem=ag_send.at[i, 0, other],
            recv_sem=ag_recv.at[i, 0, other],
            device_id=(target, code),
            device_id_type=MESH,
        )

    def hand_copy(i, other):
        block = gathered[i].at[lax.rem(dp - 2 * other + n_dp, n_dp)]
        return pltpu.make_async_remote_copy(
            src_ref=block,
            dst_ref=block,
            send_sem=ag_send.at[i, 1, other],
            recv_sem=ag_recv.at[i, 1, other],
            device_id=(partner, code),
            device_id_type=MESH,
        )

    def gather_start(i):
        for other in range(1, chips):
            peer_copy(i, other).start()
        hand_copy(i, 0).start()

    def gather_forward(i):
        for other in range(1, chips):
            peer_copy(i, other).wait_recv()
            hand_copy(i, other).start()

    def gather_finish(i):
        for other in range(1, chips):
            peer_copy(i, other).wait_send()
        for other in range(chips):
            hand_copy(i, other).wait()

    def chain_copy(way, c):
        chunk = pl.ds(pl.multiple_of(c * step_rows, step_rows), step_rows)
        src = state.at[chunk, :] if way == 0 else carry_all.at[dp, chunk, :]
        dst = (incoming, returning)[way]
        target = lax.rem(code + (1 if way == 0 else n_code - 1), n_code)
        return pltpu.make_async_remote_copy(
            src_ref=src,
            dst_ref=dst.at[chunk, :],
            send_sem=chain_send.at[way, c],
            recv_sem=chain_recv.at[way, c],
            device_id=(dp, target),
            device_id_type=MESH,
        )

    def forward_up(chunk, resid):
        size = resid.shape[0]
        base[chunk, :] = resid
        scale = lax.rsqrt(jnp.mean(resid * resid, axis=-1, keepdims=True) + EPS)
        scale_ref[chunk, :] = jnp.broadcast_to(scale, (size, 128))
        normed = (resid * scale).astype(BF16)
        normed_all[dp, chunk, :] = normed
        pre = dot_nn(normed, w1_t[...])
        pre_ref[chunk, :] = pre
        act[chunk, :] = (pre * jax.nn.sigmoid(pre)).astype(BF16)

    def forward_down(chunk):
        state[chunk, :] = (base[chunk, :] + dot_nn(act[chunk, :], w2[...])).astype(BF16)

    def backward(chunk, slope):
        slope_b = slope.astype(BF16)
        slope_all[dp, chunk, :] = slope_b
        back = dot_nn(slope_b, w2_t[...])
        pre = pre_ref[chunk, :]
        sigma = jax.nn.sigmoid(pre)
        slope_h[chunk, :] = (back * (sigma * (1.0 + pre * (1.0 - sigma)))).astype(BF16)
        norm_slope = dot_nn(slope_h[chunk, :], w1[...])
        scale = scale_ref[chunk, 0:1]
        unit = base[chunk, :] * scale
        carry_all[dp, chunk, :] = (
            slope
            + scale * (norm_slope - unit * jnp.mean(norm_slope * unit, axis=-1, keepdims=True))
        ).astype(BF16)

    def over_chunks(body):
        def turn(c, carry):
            body(c, pl.ds(pl.multiple_of(c * step_rows, step_rows), step_rows))
            return carry

        lax.fori_loop(0, CHUNKS, turn, 0)

    every = pl.ds(0, rows)

    for i in range(3):
        for way in range(2):
            ring_copy(i, way, 0).start()
    for i in range(3):
        for way in range(2):
            pass_copy(i, way, 0).start()
        own_copy(i).start()

    for load in loads:
        load.wait()
    own_rows = pl.ds(pl.multiple_of(dp * rows, 128), rows)
    vocab = table_hbm.shape[0]
    picked = lax.broadcasted_iota(jnp.int32, (vocab, rows), 0) == token[:, own_rows]
    base[...] = dot_tn(picked.astype(F32).astype(BF16), w2_t[:vocab, :width])
    line = lax.broadcasted_iota(jnp.int32, (rows, rows), 0)
    spread = lax.broadcasted_iota(jnp.int32, (rows, rows), 1)
    keep = jnp.where(line == spread, mask[...].astype(F32), 0.0).astype(BF16)
    cot_ref[...] = dot_nn(keep, cot_ref[...]).astype(BF16)

    own_copy(0).wait()
    for way in range(2):
        add_base(dp, way)
    for step in range(1, chips):
        for i in range(3):
            for way in range(2):
                ring_copy(i, way, step - 1).wait_recv()
                if step < chips - 1:
                    ring_copy(i, way, step).start()
                pass_copy(i, way, step).start()
            if i == 0:
                for way in range(2):
                    add_base(origin_of(way, step), way)
                for way in range(2):
                    pass_copy(0, way, step - 1).wait_recv()
                    add_base(origin_of(way, step - 1) + 1 - 2 * core, way)
            if i == 1 and step == chips - 1:
                for way in range(2):
                    pass_copy(0, way, chips - 1).wait_recv()
                    add_base(origin_of(way, chips - 1) + 1 - 2 * core, way)
                own_copy(1).wait()
                for way in range(2):
                    for back in range(chips):
                        pass_copy(1, way, back).wait_recv()
                flip(w1, w1_t)

    @pl.when(first)
    def _():
        forward_up(every, base[...])

    own_copy(2).wait()
    for way in range(2):
        for step in range(chips):
            pass_copy(2, way, step).wait_recv()

    @pl.when(first)
    def _():
        forward_down(every)
        for c in range(CHUNKS):
            chain_copy(0, c).start()

    for other in range(1, n_dp):
        swap_copy(0, other).start()
    cols_all[dp] = temporal[:, pl.ds(pl.multiple_of(dp * depth, 128), depth)]
    flip(w2, w2_t)

    @pl.when(jnp.logical_not(first))
    def _():
        def body(c, chunk):
            chain_copy(0, c).wait_recv()
            forward_up(chunk, base[chunk, :] + incoming[chunk, :].astype(F32))
            forward_down(chunk)

            @pl.when(jnp.logical_not(last))
            def _():
                chain_copy(0, c).start()

        over_chunks(body)

    gather_start(0)

    def send_act():
        act_t[...] = act[...].T
        for other in range(1, n_dp):
            swap_copy(1, other).start()
        act_all[:, own_rows] = act_t[pl.ds(pl.multiple_of(dp * pad, 16), pad), :]

    @pl.when(last)
    def _():
        backward(every, cot_ref[...].astype(F32))
        for c in range(CHUNKS):
            chain_copy(1, c).start()

    send_act()

    @pl.when(first)
    def _():
        gather_forward(0)

    @pl.when(jnp.logical_not(last))
    def _():
        def body(c, chunk):
            chain_copy(1, c).wait_recv()
            slope = cot_ref[chunk, :].astype(F32) + returning[chunk, :].astype(F32)
            backward(chunk, slope)

            @pl.when(jnp.logical_not(first))
            def _():
                chain_copy(1, c).start()

        over_chunks(body)

    gather_start(1)
    gather_start(2)

    @pl.when(jnp.logical_not(first))
    def _():
        gather_forward(0)

    quarter = term.shape[2]
    early = code * 2 < n_code

    def term_copy(other):
        target = lax.rem(code + other, n_code)
        return pltpu.make_async_remote_copy(
            src_ref=term.at[target],
            dst_ref=term_in.at[other],
            send_sem=term_send.at[other],
            recv_sem=term_recv.at[other],
            device_id=(dp, target),
            device_id_type=MESH,
        )

    for other in reversed(range(n_code)):
        target = lax.rem(code + other, n_code)
        spot = pl.ds(pl.multiple_of(target * quarter, 128), quarter)
        term[target] = dot_nn(carry_all[dp], proj_t[:, spot]).astype(BF16)
        if other:

            @pl.when(early)
            def _():
                term_copy(other).start()

    pre_t[...] = slope_h[...].T
    for other in range(1, n_dp):
        swap_copy(2, other).start()
    pre_all[:, own_rows] = pre_t[pl.ds(pl.multiple_of(dp * pad, 16), pad), :]

    gather_forward(1)
    gather_forward(2)

    @pl.when(jnp.logical_not(early))
    def _():
        for other in range(1, n_code):
            term_copy(other).start()

    def all_rows(array):
        return array[...].reshape(n_dp * rows, array.shape[2])

    gather_finish(0)
    gather_finish(1)
    for other in range(1, n_dp):
        swap_copy(1, other).wait()
    w2_grad[...] = dot_nn(act_all[...], all_rows(slope_all)).astype(BF16)[:share]
    for other in range(1, n_dp):
        swap_copy(2, other).wait()
    w1_grad[...] = dot_nn(pre_all[...], all_rows(normed_all)).astype(BF16)[:share]
    gather_finish(2)
    for other in range(1, n_dp):
        swap_copy(0, other).wait()
    carries = all_rows(carry_all)
    proj_grad[...] = dot_tn(all_rows(cols_all), carries).astype(BF16)
    piece = table_grad.shape[0]
    ids = lax.broadcasted_iota(jnp.int32, (piece, n_dp * rows), 0) + dp * piece
    table_grad[...] = dot_nn((ids == token[...]).astype(F32).astype(BF16), carries).astype(BF16)

    total = term[code].astype(F32)
    for other in range(1, n_code):
        term_copy(other).wait_recv()
        total += term_in[other].astype(F32)
    temporal_grad[...] = total.astype(BF16)

    for i in range(3):
        for way in range(2):
            for step in range(chips - 1):
                ring_copy(i, way, step).wait_send()
            for step in range(chips):
                pass_copy(i, way, step).wait_send()
    for c in range(CHUNKS):

        @pl.when(jnp.logical_not(last))
        def _():
            chain_copy(0, c).wait_send()

        @pl.when(jnp.logical_not(first))
        def _():
            chain_copy(1, c).wait_send()

    for other in range(1, n_code):
        term_copy(other).wait_send()


def per_device(
    temporal_out, depth_in, embed, depth_w1, depth_w2, audio_tokens, barge_mask, out_grad
):
    n_code = lax.axis_size("code")
    n_dp = lax.axis_size("dp")
    rows, wide = temporal_out.shape
    depth, width = depth_in.shape[1:]
    share = depth_w1.shape[2]
    pad = -(-share // 16) * 16
    hidden = pad * n_dp
    quarter = wide // n_code
    chips = n_dp // 2
    vocab = embed.shape[1]
    frames = audio_tokens.shape[0]
    extra = ((0, -share % 8), (0, 0))

    vmem = pl.BlockSpec(memory_space=pltpu.VMEM)
    hbm = pl.BlockSpec(memory_space=pl.ANY)
    dma = pltpu.SemaphoreType.DMA
    out_shape = (
        jax.ShapeDtypeStruct((rows, quarter), BF16),
        jax.ShapeDtypeStruct((depth, width), BF16),
        jax.ShapeDtypeStruct((vocab // n_dp, width), BF16),
        jax.ShapeDtypeStruct((share, width), BF16),
        jax.ShapeDtypeStruct((share, width), BF16),
    )
    temporal_grad, proj_grad, table_grad, w1_grad, w2_grad = pl.pallas_call(
        functools.partial(chain_kernel, n_dp, n_code),
        out_shape=out_shape,
        in_specs=[hbm] * 8,
        out_specs=(vmem,) * 5,
        scratch_shapes=[
            pltpu.VMEM((rows, wide), BF16),
            pltpu.VMEM((rows, width), BF16),
            pltpu.VMEM((1, frames), jnp.int32),
            pltpu.VMEM((1, rows), jnp.int32),
            pltpu.VMEM((wide, width), BF16),
            pltpu.VMEM((hidden, width), BF16),
            pltpu.VMEM((hidden, width), BF16),
            pltpu.VMEM((width, wide), BF16),
            pltpu.VMEM((width, hidden), BF16),
            pltpu.VMEM((width, hidden), BF16),
            pltpu.VMEM((rows, width), F32),
            pltpu.VMEM((rows, width), BF16),
            pltpu.VMEM((rows, width), BF16),
            pltpu.VMEM((rows, width), BF16),
            pltpu.VMEM((rows, hidden), F32),
            pltpu.VMEM((rows, hidden), BF16),
            pltpu.VMEM((rows, hidden), BF16),
            pltpu.VMEM((hidden, rows), BF16),
            pltpu.VMEM((hidden, rows), BF16),
            pltpu.VMEM((rows, 128), F32),
            pltpu.VMEM((n_code, rows, quarter), BF16),
            pltpu.VMEM((n_code, rows, quarter), BF16),
            pltpu.VMEM((n_dp, rows, depth), BF16),
            pltpu.VMEM((n_dp, rows, width), BF16),
            pltpu.VMEM((n_dp, rows, width), BF16),
            pltpu.VMEM((n_dp, rows, width), BF16),
            pltpu.VMEM((pad, frames), BF16),
            pltpu.VMEM((pad, frames), BF16),
            dma((5,)),
            dma((3, 2, chips)),
            dma((3, 2, chips)),
            dma((3, 2, chips)),
            dma((3, 2, chips)),
            dma((3,)),
            dma((2, CHUNKS)),
            dma((2, CHUNKS)),
            dma((3, 2, chips)),
            dma((3, 2, chips)),
            dma((3, n_dp)),
            dma((3, n_dp)),
            dma((n_code,)),
            dma((n_code,)),
        ],
        compiler_params=pltpu.CompilerParams(
            collective_id=0, has_side_effects=True, vmem_limit_bytes=63 * 1024 * 1024
        ),
        name="depth_chain",
    )(
        temporal_out,
        out_grad[:, 0, :],
        embed[0],
        audio_tokens.reshape(1, frames),
        barge_mask.reshape(1, rows),
        depth_in[0],
        jnp.pad(depth_w1[0].T, extra),
        jnp.pad(depth_w2[0].T, extra),
    )
    return (
        temporal_grad,
        proj_grad[None],
        table_grad[None],
        w1_grad.T[None],
        w2_grad.T[None],
    )


def solution(mesh):
    in_specs = (
        P("dp", None),
        P("code", "dp", None),
        P("code", None, None),
        P("code", None, "dp"),
        P("code", None, "dp"),
        P(None, "code"),
        P("dp"),
        P("dp", "code", None),
    )
    out_specs = (
        P("dp", "code"),
        P("code", "dp", None),
        P("code", "dp", None),
        P("code", None, "dp"),
        P("code", None, "dp"),
    )
    return jax.shard_map(
        per_device, mesh=mesh, in_specs=in_specs, out_specs=out_specs, check_vma=False
    )
```

time: 192 us -> 168 us (0.88)
  Pallas kernels: 172 us -> 161 us
  matrix products: 9.63 us -> 0 us
  other arithmetic: 3.16 us -> 0 us
    pallas_call x1, Pallas kernels: 172 us -> 161 us  [per_device(): pl.pallas_call(functools.partial(chain_kernel, n_dp, n_code), out_shape=o...]
    dot_general x4 -> x0, matrix products: 9.63 us -> none  [over_rows(): lax.dot_general(left, right, (((0,), (0,)), ((), ())), preferred_element_...]
    unnamed x21 -> x11, local copies, waits for them, and re-layouts: 2.81 us -> 6.34 us
where the time goes in v1:
time: 168 us
  Pallas kernels  161 us (96%)
  local copies, waits for them, and re-layouts  6.34 us (4%)
    pallas_call x1, Pallas kernels, per_device(): pl.pallas_call(functools.partial(chain_kernel, n_dp, n_code), out_shape=o...  161 us
    unnamed x11, local copies, waits for them, and re-layouts  6.34 us

profile of v1, /device:TPU:0, one launch (start us, length us, event | category | flops | bytes accessed | tf_op | source)
XLA Modules:
  0.0 167.7 jit_solution(4516212702657369413)
XLA Ops:
  0.6 160.6 %depth_chain.1 = (bf16[128,1024]{1,0:T(8,128)(2,1)}, bf16[512,1024]{1,0:T(8,128)(2,1)}, bf16[128,1024]{1,0:T(8,128)(2,1)}, bf16[264,1024]{1,0:T(8,128)(2,1)}, bf16[264,1024]{1,0:T(8,128)(2,1)}) custom-call(bf16[128,4096]{1,0:T(8,128)(2,1)} %temporal_hbm.1, bf16[128,1024]{1,0:T(8,128)(2,1)} %bitcast.26, bf16[1024,1024]{1,0:T(8,128)(2,1)} %bitcast.19, ...), custom_call_target="tpu_custom_call" | custom-call | tf_op jit(solution)/shard_map/depth_chain/pallas_call | solution.py:542
  161.3 0.0 copy-start.2
  161.3 0.0 copy-start.1
  161.3 0.0 copy-start
  161.3 1.8 %copy.18 = bf16[128,1024]{1,0:T(8,128)(2,1)} copy(bf16[128,1024]{1,0:T(8,128)(2,1)} %get-tuple-element.20) | data formatting | bytes 524288
  163.1 2.3 %copy.19 = bf16[1,512,1024]{2,1,0:T(8,128)(2,1)} copy(bf16[1,512,1024]{2,1,0:T(8,128)(2,1)} %bitcast.21) | data formatting | bytes 2097152
  165.3 0.0 copy-done.2
  165.3 0.7 copy.20
  166.0 0.0 copy-done.1
  166.1 0.8 copy.21
  166.9 0.0 copy-done
  166.9 0.8 copy.22
Async XLA Ops:
  161.3 4.1 %copy-start.2 = (bf16[128,1024]{1,0:T(8,128)(2,1)S(1)}, bf16[128,1024]{1,0:T(8,128)(2,1)}, u32[]{:S(2)}) copy-start(bf16[128,1024]{1,0:T(8,128)(2,1)} %get-tuple-element.12) | copy-start | bytes 786436
  161.3 4.8 %copy-start.1 = (bf16[264,1024]{1,0:T(8,128)(2,1)S(1)}, bf16[264,1024]{1,0:T(8,128)(2,1)}, u32[]{:S(2)}) copy-start(bf16[264,1024]{1,0:T(8,128)(2,1)} %get-tuple-element.13) | copy-start | bytes 1622020
  161.3 5.6 %copy-start = (bf16[264,1024]{1,0:T(8,128)(2,1)S(1)}, bf16[264,1024]{1,0:T(8,128)(2,1)}, u32[]{:S(2)}) copy-start(bf16[264,1024]{1,0:T(8,128)(2,1)} %get-tuple-element.14) | copy-start | bytes 1622020

commit v2 on v1

--- a/solution.py
+++ b/solution.py
@@ -32,11 +32,11 @@
     proj_own,
     w1_own,
     w2_own,
-    temporal_grad,
-    proj_grad,
-    table_grad,
-    w1_grad,
-    w2_grad,
+    temporal_out,
+    proj_out,
+    table_out,
+    w1_out,
+    w2_out,
     temporal,
     cot_ref,
     token,
@@ -65,6 +65,11 @@
     carry_all,
     act_all,
     pre_all,
+    temporal_grad,
+    proj_grad,
+    table_grad,
+    w1_grad,
+    w2_grad,
     load_sem,
     ring_send,
     ring_recv,
@@ -75,10 +80,15 @@
     chain_recv,
     ag_send,
     ag_recv,
+    hand_send,
+    hand_recv,
     swap_send,
     swap_recv,
-    term_send,
-    term_recv,
+    up_send,
+    up_recv,
+    down_send,
+    down_recv,
+    store_sem,
 ):
     dp = lax.axis_index("dp")
     code = lax.axis_index("code")
@@ -221,14 +231,14 @@
 
     gathered = (normed_all, slope_all, carry_all)
 
-    def peer_copy(i, other):
-        block = gathered[i].at[dp]
+    def peer_copy(i, other, c):
+        block = gathered[i].at[dp, pl.ds(pl.multiple_of(c * step_rows, step_rows), step_rows), :]
         target = lax.rem(dp + 2 * other, n_dp)
         return pltpu.make_async_remote_copy(
             src_ref=block,
             dst_ref=block,
-            send_sem=ag_send.at[i, 0, other],
-            recv_sem=ag_recv.at[i, 0, other],
+            send_sem=ag_send.at[i, other, c],
+            recv_sem=ag_recv.at[i, other, c],
             device_id=(target, code),
             device_id_type=MESH,
         )
@@ -238,25 +248,27 @@
         return pltpu.make_async_remote_copy(
             src_ref=block,
             dst_ref=block,
-            send_sem=ag_send.at[i, 1, other],
-            recv_sem=ag_recv.at[i, 1, other],
+            send_sem=hand_send.at[i, other],
+            recv_sem=hand_recv.at[i, other],
             device_id=(partner, code),
             device_id_type=MESH,
         )
 
-    def gather_start(i):
+    def spread(i, c):
         for other in range(1, chips):
-            peer_copy(i, other).start()
+            peer_copy(i, other, c).start()
+
+    def gather_forward(i):
         hand_copy(i, 0).start()
-
-    def gather_forward(i):
         for other in range(1, chips):
-            peer_copy(i, other).wait_recv()
+            for c in range(CHUNKS):
+                peer_copy(i, other, c).wait_recv()
             hand_copy(i, other).start()
 
     def gather_finish(i):
         for other in range(1, chips):
-            peer_copy(i, other).wait_send()
+            for c in range(CHUNKS):
+                peer_copy(i, other, c).wait_send()
         for other in range(chips):
             hand_copy(i, other).wait()
 
@@ -289,9 +301,7 @@
         state[chunk, :] = (base[chunk, :] + dot_nn(act[chunk, :], w2[...])).astype(BF16)
 
     def backward(chunk, slope):
-        slope_b = slope.astype(BF16)
-        slope_all[dp, chunk, :] = slope_b
-        back = dot_nn(slope_b, w2_t[...])
+        back = dot_nn(slope.astype(BF16), w2_t[...])
         pre = pre_ref[chunk, :]
         sigma = jax.nn.sigmoid(pre)
         slope_h[chunk, :] = (back * (sigma * (1.0 + pre * (1.0 - sigma)))).astype(BF16)
@@ -303,12 +313,8 @@
             + scale * (norm_slope - unit * jnp.mean(norm_slope * unit, axis=-1, keepdims=True))
         ).astype(BF16)
 
-    def over_chunks(body):
-        def turn(c, carry):
-            body(c, pl.ds(pl.multiple_of(c * step_rows, step_rows), step_rows))
-            return carry
-
-        lax.fori_loop(0, CHUNKS, turn, 0)
+    def rows_of(c, count):
+        return pl.ds(pl.multiple_of(c * step_rows, step_rows), count * step_rows)
 
     every = pl.ds(0, rows)
 
@@ -327,8 +333,8 @@
     picked = lax.broadcasted_iota(jnp.int32, (vocab, rows), 0) == token[:, own_rows]
     base[...] = dot_tn(picked.astype(F32).astype(BF16), w2_t[:vocab, :width])
     line = lax.broadcasted_iota(jnp.int32, (rows, rows), 0)
-    spread = lax.broadcasted_iota(jnp.int32, (rows, rows), 1)
-    keep = jnp.where(line == spread, mask[...].astype(F32), 0.0).astype(BF16)
+    column = lax.broadcasted_iota(jnp.int32, (rows, rows), 1)
+    keep = jnp.where(line == column, mask[...].astype(F32), 0.0).astype(BF16)
     cot_ref[...] = dot_nn(keep, cot_ref[...]).astype(BF16)
 
     own_copy(0).wait()
@@ -357,6 +363,64 @@
                         pass_copy(1, way, back).wait_recv()
                 flip(w1, w1_t)
 
+    quarter = term.shape[2]
+
+    def quarter_of(q):
+        return pl.ds(q * quarter, quarter)
+
+    def up_copy(q, c):
+        chunk = pl.ds(pl.multiple_of(c * step_rows, step_rows), step_rows)
+        return pltpu.make_async_remote_copy(
+            src_ref=term.at[q, chunk, :],
+            dst_ref=term_in.at[q + 1, chunk, :],
+            send_sem=up_send.at[q, c],
+            recv_sem=up_recv.at[q, c],
+            device_id=(dp, lax.rem(code + 1, n_code)),
+            device_id_type=MESH,
+        )
+
+    def down_copy(q):
+        return pltpu.make_async_remote_copy(
+            src_ref=term.at[q],
+            dst_ref=term_in.at[q],
+            send_sem=down_send.at[q],
+            recv_sem=down_recv.at[q],
+            device_id=(dp, lax.rem(code + n_code - 1, n_code)),
+            device_id_type=MESH,
+        )
+
+    def term_up(start, stop):
+        def turn(c, carry):
+            chunk = pl.ds(pl.multiple_of(c * step_rows, step_rows), step_rows)
+            for q in reversed(range(1, n_code)):
+
+                @pl.when(jnp.logical_and(jnp.logical_not(first), code <= q))
+                def _():
+                    up_copy(q, c).wait_recv()
+                    term[q, chunk, :] = (
+                        term[q, chunk, :].astype(F32) + term_in[q + 1, chunk, :].astype(F32)
+                    ).astype(BF16)
+
+                    @pl.when(code < q)
+                    def _():
+                        up_copy(q, c).start()
+
+            return carry
+
+        lax.fori_loop(start, stop, turn, 0)
+
+    def term_down():
+        for q in range(n_code - 1):
+
+            @pl.when(jnp.logical_and(jnp.logical_not(last), code >= q))
+            def _():
+                down_copy(q).wait_recv()
+                term[q] = (term[q].astype(F32) + term_in[q].astype(F32)).astype(BF16)
+
+            @pl.when(code > q)
+            def _():
+                down_copy(q).start()
+
     @pl.when(first)
     def _():
         forward_up(every, base[...])
@@ -372,39 +436,59 @@
         for c in range(CHUNKS):
             chain_copy(0, c).start()
 
+    @pl.when(first)
+    def _():
+        for c in range(CHUNKS):
+            spread(0, c)
+
+    @pl.when(last)
+    def _():
+        slope_all[dp] = cot_ref[...]
+        for c in range(CHUNKS):
+            spread(1, c)
+
     for other in range(1, n_dp):
         swap_copy(0, other).start()
     cols_all[dp] = temporal[:, pl.ds(pl.multiple_of(dp * depth, 128), depth)]
     flip(w2, w2_t)
 
-    @pl.when(jnp.logical_not(first))
-    def _():
-        def body(c, chunk):
-            chain_copy(0, c).wait_recv()
-            forward_up(chunk, base[chunk, :] + incoming[chunk, :].astype(F32))
-            forward_down(chunk)
-
-            @pl.when(jnp.logical_not(last))
-            def _():
-                chain_copy(0, c).start()
-
-        over_chunks(body)
-
-    gather_start(0)
-
-    def send_act():
-        act_t[...] = act[...].T
-        for other in range(1, n_dp):
-            swap_copy(1, other).start()
-        act_all[:, own_rows] = act_t[pl.ds(pl.multiple_of(dp * pad, 16), pad), :]
+    def forward(c):
+        chunk = rows_of(c, 1)
+        chain_copy(0, c).wait_recv()
+        forward_up(chunk, base[chunk, :] + incoming[chunk, :].astype(F32))
+        spread(0, c)
+        forward_down(chunk)
+
+    @pl.when(jnp.logical_not(jnp.logical_or(first, last)))
+    def _():
+        def turn(c, carry):
+            forward(c)
+            chain_copy(0, c).start()
+            return carry
+
+        lax.fori_loop(0, CHUNKS, turn, 0)
 
     @pl.when(last)
     def _():
-        backward(every, cot_ref[...].astype(F32))
-        for c in range(CHUNKS):
-            chain_copy(1, c).start()
-
-    send_act()
+        def turn(h, carry):
+            def inner(b, carry):
+                forward(h * 2 + b)
+                return carry
+
+            lax.fori_loop(0, 2, inner, 0)
+            pair = rows_of(h * 2, 2)
+            backward(pair, cot_ref[pair, :].astype(F32))
+            for b in range(2):
+                chain_copy(1, h * 2 + b).start()
+                spread(2, h * 2 + b)
+            return carry
+
+        lax.fori_loop(0, CHUNKS // 2, turn, 0)
+
+    act_t[...] = act[...].T
+    for other in range(1, n_dp):
+        swap_copy(1, other).start()
+    act_all[:, own_rows] = act_t[pl.ds(pl.multiple_of(dp * pad, 16), pad), :]
 
     @pl.when(first)
     def _():
@@ -412,86 +496,96 @@
 
     @pl.when(jnp.logical_not(last))
     def _():
-        def body(c, chunk):
+        def turn(c, carry):
+            chunk = rows_of(c, 1)
             chain_copy(1, c).wait_recv()
             slope = cot_ref[chunk, :].astype(F32) + returning[chunk, :].astype(F32)
+            slope_all[dp, chunk, :] = slope.astype(BF16)
+            spread(1, c)
             backward(chunk, slope)
 
             @pl.when(jnp.logical_not(first))
             def _():
                 chain_copy(1, c).start()
 
-        over_chunks(body)
-
-    gather_start(1)
-    gather_start(2)
+            spread(2, c)
+
+            @pl.when(first)
+            def _():
+                for q in reversed(range(n_code)):
+                    term[q, chunk, :] = dot_nn(
+                        carry_all[dp, chunk, :], proj_t[:, quarter_of(q)]
+                    ).astype(BF16)
+                    if q:
+                        up_copy(q, c).start()
+
+            return carry
+
+        lax.fori_loop(0, CHUNKS, turn, 0)
 
     @pl.when(jnp.logical_not(first))
     def _():
-        gather_forward(0)
-
-    quarter = term.shape[2]
-    early = code * 2 < n_code
-
-    def term_copy(other):
-        target = lax.rem(code + other, n_code)
-        return pltpu.make_async_remote_copy(
-            src_ref=term.at[target],
-            dst_ref=term_in.at[other],
-            send_sem=term_send.at[other],
-            recv_sem=term_recv.at[other],
-            device_id=(dp, target),
-            device_id_type=MESH,
-        )
-
-    for other in reversed(range(n_code)):
-        target = lax.rem(code + other, n_code)
-        spot = pl.ds(pl.multiple_of(target * quarter, 128), quarter)
-        term[target] = dot_nn(carry_all[dp], proj_t[:, spot]).astype(BF16)
-        if other:
-
-            @pl.when(early)
-            def _():
-                term_copy(other).start()
+        for q in range(n_code):
+            term[q] = dot_nn(carry_all[dp], proj_t[:, quarter_of(q)]).astype(BF16)
+            if q < n_code - 1:
+
+                @pl.when(last)
+                def _():
+                    down_copy(q).start()
 
     pre_t[...] = slope_h[...].T
     for other in range(1, n_dp):
         swap_copy(2, other).start()
     pre_all[:, own_rows] = pre_t[pl.ds(pl.multiple_of(dp * pad, 16), pad), :]
 
+    @pl.when(jnp.logical_not(first))
+    def _():
+        gather_forward(0)
+
+    term_up(0, CHUNKS // 2)
     gather_forward(1)
+    @pl.when(jnp.logical_not(last))
+    def _():
+        term_down()
+
+    term_up(CHUNKS // 2, CHUNKS)
     gather_forward(2)
-
-    @pl.when(jnp.logical_not(early))
-    def _():
-        for other in range(1, n_code):
-            term_copy(other).start()
 
     def all_rows(array):
         return array[...].reshape(n_dp * rows, array.shape[2])
 
+    def store(i):
+        pairs = (
+            (temporal_grad, temporal_out),
+            (proj_grad, proj_out),
+            (table_grad, table_out),
+            (w1_grad, w1_out),
+            (w2_grad, w2_out),
+        )
+        return pltpu.make_async_copy(pairs[i][0], pairs[i][1], store_sem.at[i])
+
+    temporal_grad[...] = term[code]
+    store(0).start()
     gather_finish(0)
     gather_finish(1)
     for other in range(1, n_dp):
         swap_copy(1, other).wait()
     w2_grad[...] = dot_nn(act_all[...], all_rows(slope_all)).astype(BF16)[:share]
-    for other in range(1, n_dp):
-        swap_copy(2, other).wait()
-    w1_grad[...] = dot_nn(pre_all[...], all_rows(normed_all)).astype(BF16)[:share]
+    store(4).start()
     gather_finish(2)
     for other in range(1, n_dp):
         swap_copy(0, other).wait()
     carries = all_rows(carry_all)
     proj_grad[...] = dot_tn(all_rows(cols_all), carries).astype(BF16)
+    store(1).start()
     piece = table_grad.shape[0]
     ids = lax.broadcasted_iota(jnp.int32, (piece, n_dp * rows), 0) + dp * piece
     table_grad[...] = dot_nn((ids == token[...]).astype(F32).astype(BF16), carries).astype(BF16)
-
-    total = term[code].astype(F32)
-    for other in range(1, n_code):
-        term_copy(other).wait_recv()
-        total += term_in[other].astype(F32)
-    temporal_grad[...] = total.astype(BF16)
+    store(2).start()
+    for other in range(1, n_dp):
+        swap_copy(2, other).wait()
+    w1_grad[...] = dot_nn(pre_all[...], all_rows(normed_all)).astype(BF16)[:share]
+    store(3).start()
 
     for i in range(3):
         for way in range(2):
@@ -509,8 +603,32 @@
         def _():
             chain_copy(1, c).wait_send()
 
-    for other in range(1, n_code):
-        term_copy(other).wait_send()
+    for q in range(n_code):
+
+        @pl.when(code < q)
+        def _():
+            for c in range(CHUNKS):
+                up_copy(q, c).wait_send()
+
+        @pl.when(code > q)
+        def _():
+            down_copy(q).wait_send()
+
+    for i in range(5):
+        store(i).wait()
+
+
+def copy_kernel(*refs):
+    sources, targets, slots, (in_sem, out_sem) = refs[:5], refs[5:10], refs[10:15], refs[15:]
+    takes = [pltpu.make_async_copy(sources[i], slots[i], in_sem.at[i]) for i in range(5)]
+    gives = [pltpu.make_async_copy(slots[i], targets[i], out_sem.at[i]) for i in range(5)]
+    for take in takes:
+        take.start()
+    for take, give in zip(takes, gives):
+        take.wait()
+        give.start()
+    for give in gives:
+        give.wait()
 
 
 def per_device(
@@ -529,7 +647,6 @@
     frames = audio_tokens.shape[0]
     extra = ((0, -share % 8), (0, 0))
 
-    vmem = pl.BlockSpec(memory_space=pltpu.VMEM)
     hbm = pl.BlockSpec(memory_space=pl.ANY)
     dma = pltpu.SemaphoreType.DMA
     out_shape = (
@@ -539,11 +656,11 @@
         jax.ShapeDtypeStruct((share, width), BF16),
         jax.ShapeDtypeStruct((share, width), BF16),
     )
-    temporal_grad, proj_grad, table_grad, w1_grad, w2_grad = pl.pallas_call(
+    results = pl.pallas_call(
         functools.partial(chain_kernel, n_dp, n_code),
         out_shape=out_shape,
         in_specs=[hbm] * 8,
-        out_specs=(vmem,) * 5,
+        out_specs=(hbm,) * 5,
         scratch_shapes=[
             pltpu.VMEM((rows, wide), BF16),
             pltpu.VMEM((rows, width), BF16),
@@ -566,13 +683,14 @@
             pltpu.VMEM((hidden, rows), BF16),
             pltpu.VMEM((rows, 128), F32),
             pltpu.VMEM((n_code, rows, quarter), BF16),
-            pltpu.VMEM((n_code, rows, quarter), BF16),
+            pltpu.VMEM((n_code + 1, rows, quarter), BF16),
             pltpu.VMEM((n_dp, rows, depth), BF16),
             pltpu.VMEM((n_dp, rows, width), BF16),
             pltpu.VMEM((n_dp, rows, width), BF16),
             pltpu.VMEM((n_dp, rows, width), BF16),
             pltpu.VMEM((pad, frames), BF16),
             pltpu.VMEM((pad, frames), BF16),
+            *(pltpu.VMEM(leaf.shape, BF16) for leaf in out_shape),
             dma((5,)),
             dma((3, 2, chips)),
             dma((3, 2, chips)),
@@ -581,12 +699,17 @@
             dma((3,)),
             dma((2, CHUNKS)),
             dma((2, CHUNKS)),
-            dma((3, 2, chips)),
-            dma((3, 2, chips)),
+            dma((3, chips, CHUNKS)),
+            dma((3, chips, CHUNKS)),
+            dma((3, chips)),
+            dma((3, chips)),
             dma((3, n_dp)),
             dma((3, n_dp)),
+            dma((n_code, CHUNKS)),
+            dma((n_code, CHUNKS)),
             dma((n_code,)),
             dma((n_code,)),
+            dma((5,)),
         ],
         compiler_params=pltpu.CompilerParams(
             collective_id=0, has_side_effects=True, vmem_limit_bytes=63 * 1024 * 1024
@@ -602,6 +725,18 @@
         jnp.pad(depth_w1[0].T, extra),
         jnp.pad(depth_w2[0].T, extra),
     )
+    temporal_grad, proj_grad, table_grad, w1_grad, w2_grad = pl.pallas_call(
+        copy_kernel,
+        out_shape=out_shape,
+        in_specs=[hbm] * 5,
+        out_specs=(hbm,) * 5,
+        scratch_shapes=[
+            *(pltpu.VMEM(leaf.shape, BF16) for leaf in out_shape),
+            dma((5,)),
+            dma((5,)),
+        ],
+        name="results",
+    )(*results)
     return (
         temporal_grad,
         proj_grad[None],

time: 168 us -> 160 us (0.952)
  the two profiles are of different devices: /device:TPU:0 before, /device:TPU:27 now
where the time goes in v2:
time: 160 us
  Pallas kernels  159 us (99%)
    pallas_call x1, Pallas kernels, per_device(): pl.pallas_call(functools.partial(chain_kernel, n_dp, n_code), out_shape=o...  157 us

profile of v2, /device:TPU:27, one launch (start us, length us, event | category | flops | bytes accessed | tf_op | source)
XLA Modules:
  0.0 160.1 jit_solution(4838034189747738419)
XLA Ops:
  0.6 156.5 %depth_chain.1 = (bf16[128,1024]{1,0:T(8,128)(2,1)}, bf16[512,1024]{1,0:T(8,128)(2,1)}, bf16[128,1024]{1,0:T(8,128)(2,1)}, bf16[264,1024]{1,0:T(8,128)(2,1)}, bf16[264,1024]{1,0:T(8,128)(2,1)}) custom-call(bf16[128,4096]{1,0:T(8,128)(2,1)} %temporal_hbm.1, bf16[128,1024]{1,0:T(8,128)(2,1)} %bitcast.23, bf16[1024,1024]{1,0:T(8,128)(2,1)} %bitcast.19, ...), custom_call_target="tpu_custom_call" | custom-call | tf_op jit(solution)/shard_map/depth_chain/pallas_call | solution.py:659
  157.1 2.8 %results.1 = (bf16[128,1024]{1,0:T(8,128)(2,1)}, bf16[512,1024]{1,0:T(8,128)(2,1)}, bf16[128,1024]{1,0:T(8,128)(2,1)}, bf16[264,1024]{1,0:T(8,128)(2,1)}, bf16[264,1024]{1,0:T(8,128)(2,1)}) custom-call(bf16[128,1024]{1,0:T(8,128)(2,1)} %get-tuple-element.15.refs_0_, bf16[512,1024]{1,0:T(8,128)(2,1)} %get-tuple-element.16.refs_1_, ...), custom_call_target="tpu_custom_call" | custom-call | tf_op jit(solution)/shard_map/results/pallas_call | solution.py:728
